TPU v7x, 32 devices: a whole 2x2x4 slice. The times are simulated.
32 devices in a mesh: section: 4 (over z), seq: 8 (over y, x, core).
Axes of the slice: x: 2, y: 2, z: 4, core: 2. Of those that a mesh axis runs over, the one named last changes fastest.
Arguments:
- queries: bfloat16 [4, 2, 1024, 4096], P('section', None, 'seq'), may hold values from -80 to 80
- keys_new: bfloat16 [4, 2, 1024, 1024], P('section', None, 'seq'), may hold values from -4 to 4
- values_new: bfloat16 [4, 2, 1024, 1024], P('section', None, 'seq'), may hold values from -6 to 6
- key_cache: bfloat16 [4, 32, 4096, 128], P('section', 'seq'), may hold values from -6 to 6
- value_cache: bfloat16 [4, 32, 4096, 128], P('section', 'seq'), may hold values from -6 to 6
- block_lists: int32 [4, 32, 2, 16, 32], P('section', 'seq'), may hold values from 0 to 63, as said below
- block_counts: int32 [4, 32, 2, 16], P('section', 'seq'), may hold values from 1 to 32
- visible_blocks: int32 [2], replicated, may hold values from 32 to 64
Outputs:
- handed: bfloat16 [4, 2, 1024, 4096], P('section', None, 'seq')
Inputs may be any that keep to these rules, and one draw needn't show every extreme that they name: `block_lists`: each list holds 32 different block numbers.
All inputs are finite; a program needn't handle non-finite values.
Results may differ from a plain program's by a relative error of at most 0.003.
Values may be sent and summed in bfloat16 or wider, within the bound.
A program may use at most 192 MiB of HBM per device.

v0:
```python
import jax
import jax.numpy as jnp
from jax import lax
from jax.sharding import PartitionSpec as P

HEADS = 32
KVH = 8
DH = 128
BLK = 64


select_group = 8


def shifted(block, axis, distance):
    devices = range(lax.axis_size(axis))
    route = [((i - distance) % len(devices), i) for i in devices]
    return lax.ppermute(block, axis, route)


def pick_blocks(table, chosen):
    return table[chosen]


def attend(
    query_local,
    key_local,
    value_local,
    cache_keys,
    cache_values,
    lists_span,
    counts_span,
    visible_count,
):
    span_len, heads_dev, head_dim = query_local.shape
    block_len = cache_keys.shape[2]
    query_blocks = span_len // block_len
    score_scale = 1.0 / head_dim**0.5
    own_scores = (
        jnp.einsum("rhd,khd->rhk", query_local, key_local, preferred_element_type=jnp.float32)
        * score_scale
    )
    causal = jnp.arange(span_len)[:, None] >= jnp.arange(span_len)[None, :]
    own_scores = jnp.where(causal[:, None, :], own_scores, -jnp.inf)
    row_max = jnp.max(own_scores, axis=2)
    own_weights = jnp.exp(own_scores - row_max[:, :, None])
    row_sum = jnp.sum(own_weights, axis=2)
    weighted = jnp.einsum(
        "rhk,khd->rhd",
        own_weights.astype(jnp.bfloat16),
        value_local,
        preferred_element_type=jnp.float32,
    )
    row_max = row_max.reshape(query_blocks, block_len, heads_dev)
    row_sum = row_sum.reshape(query_blocks, block_len, heads_dev)
    weighted = weighted.reshape(query_blocks, block_len, heads_dev, head_dim)
    query_tiles = query_local.reshape(query_blocks, block_len, heads_dev, head_dim)
    rounds = (jnp.max(counts_span) + select_group - 1) // select_group

    def one_round(step_index, carry):
        run_max, run_sum, run_weighted = carry
        chosen = lax.dynamic_slice_in_dim(
            lists_span, step_index * select_group, select_group, axis=2
        )
        slot_index = step_index * select_group + jnp.arange(select_group)
        usable = (slot_index[None, None, :] < counts_span[:, :, None]) & (chosen < visible_count)
        key_blocks = jax.vmap(pick_blocks)(cache_keys, chosen)
        value_blocks = jax.vmap(pick_blocks)(cache_values, chosen)
        scores = (
            jnp.einsum(
                "qbhd,hqgtd->qbhgt", query_tiles, key_blocks, preferred_element_type=jnp.float32
            )
            * score_scale
        )
        usable_view = jnp.transpose(usable, (1, 0, 2))[:, None, :, :, None]
        scores = jnp.where(usable_view, scores, -jnp.inf)
        new_max = jnp.maximum(run_max, jnp.max(scores, axis=(3, 4)))
        carry_scale = jnp.exp(run_max - new_max)
        weights = jnp.exp(scores - new_max[:, :, :, None, None])
        new_sum = run_sum * carry_scale + jnp.sum(weights, axis=(3, 4))
        new_weighted = run_weighted * carry_scale[:, :, :, None] + jnp.einsum(
            "qbhgt,hqgtd->qbhd",
            weights.astype(jnp.bfloat16),
            value_blocks,
            preferred_element_type=jnp.float32,
        )
        return (new_max, new_sum, new_weighted)

    run_max, run_sum, run_weighted = lax.fori_loop(
        0, rounds, one_round, (row_max, row_sum, weighted)
    )
    finished = (run_weighted / run_sum[:, :, :, None]).astype(jnp.bfloat16)
    return finished.reshape(span_len, heads_dev, head_dim)


def on_device(
    queries, keys_new, values_new, key_cache, value_cache, block_lists, block_counts, visible_blocks
):
    span_count = queries.shape[1]
    row_count = queries.shape[2]
    group_size = HEADS // KVH
    query_rows = queries[0].reshape(span_count, row_count, HEADS, DH)

    def spread_heads(source):
        shaped = source[0].reshape(span_count, row_count, KVH, 1, DH)
        return jnp.broadcast_to(shaped, (span_count, row_count, KVH, group_size, DH)).reshape(
            span_count, row_count, HEADS, DH
        )

    key_rows = spread_heads(keys_new)
    value_rows = spread_heads(values_new)
    heads_dev = key_cache.shape[1]
    cache_blocks_total = key_cache.shape[2] // BLK
    cache_keys = key_cache[0].reshape(heads_dev, cache_blocks_total, BLK, DH)
    cache_values = value_cache[0].reshape(heads_dev, cache_blocks_total, BLK, DH)
    lists_local = block_lists[0]
    counts_local = block_counts[0]
    attended = []
    query_all, key_all, value_all = (
        lax.all_to_all(query_rows, "seq", split_axis=2, concat_axis=1, tiled=True),
        lax.all_to_all(key_rows, "seq", split_axis=2, concat_axis=1, tiled=True),
        lax.all_to_all(value_rows, "seq", split_axis=2, concat_axis=1, tiled=True),
    )
    for span_index in range(span_count):
        attended.append(
            attend(
                query_all[span_index],
                key_all[span_index],
                value_all[span_index],
                cache_keys,
                cache_values,
                lists_local[:, span_index],
                counts_local[:, span_index],
                visible_blocks[span_index],
            )
        )
    result = jnp.stack(attended)
    returned_here = lax.all_to_all(result, "seq", split_axis=1, concat_axis=2, tiled=True)
    returned = shifted(returned_here, "section", 1)
    return returned.reshape(1, span_count, row_count, HEADS * DH)


def solution(mesh):
    return jax.shard_map(
        on_device,
        mesh=mesh,
        in_specs=(
            P("section", None, "seq", None),
            P("section", None, "seq", None),
            P("section", None, "seq", None),
            P("section", "seq", None, None),
            P("section", "seq", None, None),
            P("section", "seq", None, None, None),
            P("section", "seq", None, None),
            P(),
        ),
        out_specs=P("section", None, "seq", None),
        check_vma=False,
    )
```

profile of v0, /device:TPU:0, one launch (start us, length us, event | category | flops | bytes accessed | tf_op | source)
XLA Modules:
  0.0 593.3 jit_solution(2181194268830075936)
XLA Ops:
  0.0 3.1 copy.148
  4.6 5.3 all-to-all-start.1
  11.2 25.4 %all-to-all-done.1 = bf16[2,128,32,128]{1,3,0,2:T(8,128)(2,1)S(1)} async-done(((bf16[2,128,32,128]{1,3,0,2:T(8,128)(2,1)}), bf16[2,128,32,128]{1,3,0,2:T(8,128)(2,1)S(1)}, u32[]{:S(2)}, u32[]{:S(2)}) %all-to-all-start.1) | async-done | bytes 2097184 | tf_op jit(solution)/shard_map/all_to_all | solution.py:120
  36.6 1.8 broadcast_in_dim.80
  38.4 4.3 all-to-all-start
  49.0 2.9 copy.150
  51.9 2.7 fusion.65
  54.6 14.7 %all-to-all-done = bf16[2,128,32,128]{3,1,0,2:T(8,128)(2,1)} async-done(((bf16[2,128,32,128]{3,1,0,2:T(8,128)(2,1)}), bf16[2,128,32,128]{3,1,0,2:T(8,128)(2,1)}, u32[]{:S(2)}, u32[]{:S(2)}) %all-to-all-start) | async-done | bytes 2097184 | tf_op jit(solution)/shard_map/all_to_all | solution.py:121
  69.4 2.9 broadcast_in_dim.83
  72.2 4.5 all-to-all-start.2
  78.8 7.3 %fusion.50 = (f32[1024,4]{0,1:T(4,128)S(1)}, f32[4,1024,1024]{2,1,0:T(8,128)}) fusion(pred[1024,1024]{0,1:T(8,128)(4,1)S(1)} %iota_compare_fusion, bf16[1024,4,128]{2,0,1:T(8,128)(2,1)S(1)} %bitcast.256, bf16[1024,4,128]{2,0,1:T(8,128)(2,1)S(1)} %bitcast.247), kind=kOutput, calls=%fused_computation.66 | convolution fusion | flops 1086320640 | bytes 19939328 | tf_op jit(solution)/shard_map/rhd,khd->rhk/dot_general | solution.py:40
  87.4 13.9 %fusion.47 = (f32[1024,4]{0,1:T(4,128)S(1)}, f32[1024,4]{0,1:T(4,128)}, f32[4,1024,1024]{2,1,0:T(8,128)}) fusion(f32[4,1024,1024]{2,1,0:T(8,128)} %get-tuple-element.306, f32[1024,4]{0,1:T(4,128)S(1)} %get-tuple-element.305, pred[1024,1024]{0,1:T(8,128)(4,1)S(1)} %iota_compare_fusion, bf16[1024,4,128]{2,0,1:T(8,128)(2,1)} %bitcast.275, ...), kind=kOutput, calls=%fused_computation.63 | convolution fusion | flops 1103093760 | bytes 36749312 | tf_op jit(solution)/shard_map/rhd,khd->rhk/dot_general | solution.py:40
  101.4 2.0 all-to-all-done.2
  106.3 12.3 %fusion.54 = f32[4,1024,128]{2,1,0:T(8,128)} fusion(bf16[1024,4,128]{2,0,1:T(8,128)(2,1)S(1)} %bitcast.276, f32[4,1024,1024]{2,1,0:T(8,128)} %get-tuple-element.306, f32[1024,4]{0,1:T(4,128)S(1)} %get-tuple-element.305, pred[1024,1024]{0,1:T(8,128)(4,1)S(1)} %iota_compare_fusion), kind=kOutput, calls=%fused_computation.69 | convolution fusion | flops 1090519040 | bytes 20987904 | tf_op jit(solution)/shard_map/rhk,khd->rhd/dot_general | solution.py:48
  118.6 3.2 copy.160
  122.9 181.6 %while.28 = (s32[]{:T(128)}, f32[16,64,4]{1,2,0:T(4,128)S(1)}, f32[16,64,4]{1,2,0:T(4,128)S(1)}, f32[16,64,4,128]{3,1,2,0:T(8,128)}, s32[]{:T(128)}, /*index=5*/...) while((s32[]{:T(128)}, f32[16,64,4]{1,2,0:T(4,128)S(1)}, ...), condition=%wide.region_6.7_spmd, body=%wide.region_3.6_spmd.sunk | while | flops 1097872896 | bytes 131356248 | solution.py:89
  124.0 9.8 %gather_fusion = bf16[512,64,128]{2,1,0:T(8,128)(2,1)} fusion(bf16[4,64,64,128]{3,2,1,0:T(8,128)(2,1)} %get-tuple-element.551, s32[512]{0:T(512)S(1)} %reshape.135), kind=kCustom, calls=%fused_computation.clone.1 | custom fusion | bytes 16781312 | tf_op jit(solution)/shard_map/while/body/vmap()/gather | solution.py:22
  133.8 6.2 %bitcast_reduce_fusion.4 = (f32[16,64,4]{1,2,0:T(4,128)S(1)}, f32[16,4,8,64,64]{4,3,2,1,0:T(8,128)S(1)}) fusion(pred[16,4,8]{2,1,0:T(4,128)(4,1)S(1)} %copy.224, bf16[16,64,4,128]{3,1,2,0:T(8,128)(2,1)} %get-tuple-element.552, bf16[4,16,8,64,128]{4,3,2,1,0:T(8,128)(2,1)} %bitcast.243), kind=kOutput, calls=%fused_computation.5.clone.1 | convolution fusion | flops 543158272 | bytes 17842688 | tf_op jit(solution)/shard_map/while/body/qbhd,hqgtd->qbhgt/dot_general | solution.py:70
  140.0 4.5 fusion.85
  145.8 10.0 %gather_fusion.1 = bf16[512,64,128]{2,1,0:T(8,128)(2,1)} fusion(bf16[4,64,64,128]{3,2,1,0:T(8,128)(2,1)} %get-tuple-element.553, s32[512]{0:T(512)S(1)} %reshape.135), kind=kCustom, calls=%fused_computation.1.clone.1 | custom fusion | bytes 16781312 | tf_op jit(solution)/shard_map/while/body/vmap()/gather | solution.py:22
  155.8 11.4 %bitcast_add_fusion.4 = f32[16,64,4,128]{3,1,2,0:T(8,128)S(1)} fusion(f32[16,64,4,128]{3,1,2,0:T(8,128)S(1)} %copy-done.4, f32[16,4,8,64,64]{4,3,2,1,0:T(8,128)} %copy-done, f32[16,64,4]{1,2,0:T(4,128)S(1)} %max.8, pred[16,4,8]{2,1,0:T(4,128)(4,1)S(1)} %copy.224, bf16[4,16,8,64,128]{4,3,2,1,0:T(8,128)(2,1)} %bitcast.241, f32[16,64,4]{1,2,0:T(4,128)S(1)} %bitcast.277), kind=kOutput, calls=%fused_computation.18.clone.1 | convolution fusion | flops 546308096 | bytes 21004800 | tf_op jit(solution)/shard_map/while/body/qbhgt,hqgtd->qbhd/dot_general | solution.py:81
  169.4 9.8 %gather_fusion = bf16[512,64,128]{2,1,0:T(8,128)(2,1)} fusion(bf16[4,64,64,128]{3,2,1,0:T(8,128)(2,1)} %get-tuple-element.551, s32[512]{0:T(512)S(1)} %reshape.135), kind=kCustom, calls=%fused_computation.clone.1 | custom fusion | bytes 16781312 | tf_op jit(solution)/shard_map/while/body/vmap()/gather | solution.py:22
  179.2 6.2 %bitcast_reduce_fusion.4 = (f32[16,64,4]{1,2,0:T(4,128)S(1)}, f32[16,4,8,64,64]{4,3,2,1,0:T(8,128)S(1)}) fusion(pred[16,4,8]{2,1,0:T(4,128)(4,1)S(1)} %copy.224, bf16[16,64,4,128]{3,1,2,0:T(8,128)(2,1)} %get-tuple-element.552, bf16[4,16,8,64,128]{4,3,2,1,0:T(8,128)(2,1)} %bitcast.243), kind=kOutput, calls=%fused_computation.5.clone.1 | convolution fusion | flops 543158272 | bytes 17842688 | tf_op jit(solution)/shard_map/while/body/qbhd,hqgtd->qbhgt/dot_general | solution.py:70
  185.4 4.5 fusion.85
  191.1 10.0 %gather_fusion.1 = bf16[512,64,128]{2,1,0:T(8,128)(2,1)} fusion(bf16[4,64,64,128]{3,2,1,0:T(8,128)(2,1)} %get-tuple-element.553, s32[512]{0:T(512)S(1)} %reshape.135), kind=kCustom, calls=%fused_computation.1.clone.1 | custom fusion | bytes 16781312 | tf_op jit(solution)/shard_map/while/body/vmap()/gather | solution.py:22
  201.1 11.4 %bitcast_add_fusion.4 = f32[16,64,4,128]{3,1,2,0:T(8,128)S(1)} fusion(f32[16,64,4,128]{3,1,2,0:T(8,128)S(1)} %copy-done.4, f32[16,4,8,64,64]{4,3,2,1,0:T(8,128)} %copy-done, f32[16,64,4]{1,2,0:T(4,128)S(1)} %max.8, pred[16,4,8]{2,1,0:T(4,128)(4,1)S(1)} %copy.224, bf16[4,16,8,64,128]{4,3,2,1,0:T(8,128)(2,1)} %bitcast.241, f32[16,64,4]{1,2,0:T(4,128)S(1)} %bitcast.277), kind=kOutput, calls=%fused_computation.18.clone.1 | convolution fusion | flops 546308096 | bytes 21004800 | tf_op jit(solution)/shard_map/while/body/qbhgt,hqgtd->qbhd/dot_general | solution.py:81
  214.7 9.8 %gather_fusion = bf16[512,64,128]{2,1,0:T(8,128)(2,1)} fusion(bf16[4,64,64,128]{3,2,1,0:T(8,128)(2,1)} %get-tuple-element.551, s32[512]{0:T(512)S(1)} %reshape.135), kind=kCustom, calls=%fused_computation.clone.1 | custom fusion | bytes 16781312 | tf_op jit(solution)/shard_map/while/body/vmap()/gather | solution.py:22
  224.5 6.2 %bitcast_reduce_fusion.4 = (f32[16,64,4]{1,2,0:T(4,128)S(1)}, f32[16,4,8,64,64]{4,3,2,1,0:T(8,128)S(1)}) fusion(pred[16,4,8]{2,1,0:T(4,128)(4,1)S(1)} %copy.224, bf16[16,64,4,128]{3,1,2,0:T(8,128)(2,1)} %get-tuple-element.552, bf16[4,16,8,64,128]{4,3,2,1,0:T(8,128)(2,1)} %bitcast.243), kind=kOutput, calls=%fused_computation.5.clone.1 | convolution fusion | flops 543158272 | bytes 17842688 | tf_op jit(solution)/shard_map/while/body/qbhd,hqgtd->qbhgt/dot_general | solution.py:70
  230.7 4.5 fusion.85
  236.4 10.0 %gather_fusion.1 = bf16[512,64,128]{2,1,0:T(8,128)(2,1)} fusion(bf16[4,64,64,128]{3,2,1,0:T(8,128)(2,1)} %get-tuple-element.553, s32[512]{0:T(512)S(1)} %reshape.135), kind=kCustom, calls=%fused_computation.1.clone.1 | custom fusion | bytes 16781312 | tf_op jit(solution)/shard_map/while/body/vmap()/gather | solution.py:22
  246.4 11.4 %bitcast_add_fusion.4 = f32[16,64,4,128]{3,1,2,0:T(8,128)S(1)} fusion(f32[16,64,4,128]{3,1,2,0:T(8,128)S(1)} %copy-done.4, f32[16,4,8,64,64]{4,3,2,1,0:T(8,128)} %copy-done, f32[16,64,4]{1,2,0:T(4,128)S(1)} %max.8, pred[16,4,8]{2,1,0:T(4,128)(4,1)S(1)} %copy.224, bf16[4,16,8,64,128]{4,3,2,1,0:T(8,128)(2,1)} %bitcast.241, f32[16,64,4]{1,2,0:T(4,128)S(1)} %bitcast.277), kind=kOutput, calls=%fused_computation.18.clone.1 | convolution fusion | flops 546308096 | bytes 21004800 | tf_op jit(solution)/shard_map/while/body/qbhgt,hqgtd->qbhd/dot_general | solution.py:81
  260.0 9.8 %gather_fusion = bf16[512,64,128]{2,1,0:T(8,128)(2,1)} fusion(bf16[4,64,64,128]{3,2,1,0:T(8,128)(2,1)} %get-tuple-element.551, s32[512]{0:T(512)S(1)} %reshape.135), kind=kCustom, calls=%fused_computation.clone.1 | custom fusion | bytes 16781312 | tf_op jit(solution)/shard_map/while/body/vmap()/gather | solution.py:22
  269.8 6.2 %bitcast_reduce_fusion.4 = (f32[16,64,4]{1,2,0:T(4,128)S(1)}, f32[16,4,8,64,64]{4,3,2,1,0:T(8,128)S(1)}) fusion(pred[16,4,8]{2,1,0:T(4,128)(4,1)S(1)} %copy.224, bf16[16,64,4,128]{3,1,2,0:T(8,128)(2,1)} %get-tuple-element.552, bf16[4,16,8,64,128]{4,3,2,1,0:T(8,128)(2,1)} %bitcast.243), kind=kOutput, calls=%fused_computation.5.clone.1 | convolution fusion | flops 543158272 | bytes 17842688 | tf_op jit(solution)/shard_map/while/body/qbhd,hqgtd->qbhgt/dot_general | solution.py:70
  276.0 4.5 fusion.85
  281.7 10.0 %gather_fusion.1 = bf16[512,64,128]{2,1,0:T(8,128)(2,1)} fusion(bf16[4,64,64,128]{3,2,1,0:T(8,128)(2,1)} %get-tuple-element.553, s32[512]{0:T(512)S(1)} %reshape.135), kind=kCustom, calls=%fused_computation.1.clone.1 | custom fusion | bytes 16781312 | tf_op jit(solution)/shard_map/while/body/vmap()/gather | solution.py:22
  291.7 11.4 %bitcast_add_fusion.4 = f32[16,64,4,128]{3,1,2,0:T(8,128)S(1)} fusion(f32[16,64,4,128]{3,1,2,0:T(8,128)S(1)} %copy-done.4, f32[16,4,8,64,64]{4,3,2,1,0:T(8,128)} %copy-done, f32[16,64,4]{1,2,0:T(4,128)S(1)} %max.8, pred[16,4,8]{2,1,0:T(4,128)(4,1)S(1)} %copy.224, bf16[4,16,8,64,128]{4,3,2,1,0:T(8,128)(2,1)} %bitcast.241, f32[16,64,4]{1,2,0:T(4,128)S(1)} %bitcast.277), kind=kOutput, calls=%fused_computation.18.clone.1 | convolution fusion | flops 546308096 | bytes 21004800 | tf_op jit(solution)/shard_map/while/body/qbhgt,hqgtd->qbhd/dot_general | solution.py:81
  306.5 7.7 %fusion.49 = f32[1024,4]{0,1:T(4,128)S(1)} fusion(f32[4,1024,1024]{2,1,0:T(8,128)} %get-tuple-element.307, f32[1024,4]{0,1:T(4,128)S(1)} %copy-done.14, pred[1024,1024]{0,1:T(8,128)(4,1)S(1)} %copy-done.3), kind=kLoop, calls=%fused_computation.65 | loop fusion | flops 16773120 | bytes 17858560 | tf_op jit(solution)/shard_map/reduce_sum | solution.py:47
  314.3 12.3 %fusion.52 = f32[4,1024,128]{2,1,0:T(8,128)} fusion(bf16[1024,4,128]{2,0,1:T(8,128)(2,1)S(1)} %bitcast.274, f32[4,1024,1024]{2,1,0:T(8,128)} %get-tuple-element.307, f32[1024,4]{0,1:T(4,128)S(1)} %copy-done.14, pred[1024,1024]{0,1:T(8,128)(4,1)S(1)} %copy-done.3), kind=kOutput, calls=%fused_computation.68 | convolution fusion | flops 1090519040 | bytes 20987904 | tf_op jit(solution)/shard_map/rhk,khd->rhd/dot_general | solution.py:48
  329.6 174.6 %while.29 = (s32[]{:T(128)}, f32[16,64,4]{1,2,0:T(4,128)S(1)}, f32[16,64,4]{1,2,0:T(4,128)S(1)}, f32[16,64,4,128]{3,1,2,0:T(8,128)S(1)}, s32[]{:T(128)}, /*index...) while((s32[]{:T(128)}, f32[16,64,4]{1,2,0:T(4,128)S(1)}, ...), condition=%wide.region_13.14_spmd, body=%wide.region_10.13_spmd.sunk | while | flops 1097872896 | bytes 118773320 | solution.py:89
  330.8 9.9 %gather_fusion.2 = bf16[512,64,128]{2,1,0:T(8,128)(2,1)} fusion(bf16[4,64,64,128]{3,2,1,0:T(8,128)(2,1)} %get-tuple-element.506, s32[512]{0:T(512)S(1)} %reshape.140), kind=kCustom, calls=%fused_computation.2.clone.1 | custom fusion | bytes 16781312 | tf_op jit(solution)/shard_map/while/body/vmap()/gather | solution.py:22
  340.7 5.7 bitcast_reduce_fusion.5
  346.4 4.5 fusion.89
  352.1 9.8 %gather_fusion.3 = bf16[512,64,128]{2,1,0:T(8,128)(2,1)} fusion(bf16[4,64,64,128]{3,2,1,0:T(8,128)(2,1)} %get-tuple-element.508, s32[512]{0:T(512)S(1)} %reshape.140), kind=kCustom, calls=%fused_computation.3.clone.1 | custom fusion | bytes 16781312 | tf_op jit(solution)/shard_map/while/body/vmap()/gather | solution.py:22
  361.9 11.4 %bitcast_add_fusion.5 = f32[16,64,4,128]{3,1,2,0:T(8,128)S(1)} fusion(f32[16,64,4,128]{3,1,2,0:T(8,128)S(1)} %get-tuple-element.486, f32[16,4,8,64,64]{4,3,2,1,0:T(8,128)} %copy-done.1, f32[16,64,4]{1,2,0:T(4,128)S(1)} %max.9, pred[16,4,8]{2,1,0:T(4,128)(4,1)S(1)} %copy.227, bf16[4,16,8,64,128]{4,3,2,1,0:T(8,128)(2,1)} %bitcast.242, ...), kind=kOutput, calls=%fused_computation.45.clone.1 | convolution fusion | flops 546308096 | bytes 21004800 | tf_op jit(solution)/shard_map/while/body/qbhgt,hqgtd->qbhd/dot_general | solution.py:81
  374.3 9.9 %gather_fusion.2 = bf16[512,64,128]{2,1,0:T(8,128)(2,1)} fusion(bf16[4,64,64,128]{3,2,1,0:T(8,128)(2,1)} %get-tuple-element.506, s32[512]{0:T(512)S(1)} %reshape.140), kind=kCustom, calls=%fused_computation.2.clone.1 | custom fusion | bytes 16781312 | tf_op jit(solution)/shard_map/while/body/vmap()/gather | solution.py:22
  384.2 5.7 bitcast_reduce_fusion.5
  390.0 4.5 fusion.89
  395.7 9.8 %gather_fusion.3 = bf16[512,64,128]{2,1,0:T(8,128)(2,1)} fusion(bf16[4,64,64,128]{3,2,1,0:T(8,128)(2,1)} %get-tuple-element.508, s32[512]{0:T(512)S(1)} %reshape.140), kind=kCustom, calls=%fused_computation.3.clone.1 | custom fusion | bytes 16781312 | tf_op jit(solution)/shard_map/while/body/vmap()/gather | solution.py:22
  405.5 11.4 %bitcast_add_fusion.5 = f32[16,64,4,128]{3,1,2,0:T(8,128)S(1)} fusion(f32[16,64,4,128]{3,1,2,0:T(8,128)S(1)} %get-tuple-element.486, f32[16,4,8,64,64]{4,3,2,1,0:T(8,128)} %copy-done.1, f32[16,64,4]{1,2,0:T(4,128)S(1)} %max.9, pred[16,4,8]{2,1,0:T(4,128)(4,1)S(1)} %copy.227, bf16[4,16,8,64,128]{4,3,2,1,0:T(8,128)(2,1)} %bitcast.242, ...), kind=kOutput, calls=%fused_computation.45.clone.1 | convolution fusion | flops 546308096 | bytes 21004800 | tf_op jit(solution)/shard_map/while/body/qbhgt,hqgtd->qbhd/dot_general | solution.py:81
  417.9 9.9 %gather_fusion.2 = bf16[512,64,128]{2,1,0:T(8,128)(2,1)} fusion(bf16[4,64,64,128]{3,2,1,0:T(8,128)(2,1)} %get-tuple-element.506, s32[512]{0:T(512)S(1)} %reshape.140), kind=kCustom, calls=%fused_computation.2.clone.1 | custom fusion | bytes 16781312 | tf_op jit(solution)/shard_map/while/body/vmap()/gather | solution.py:22
  427.8 5.7 bitcast_reduce_fusion.5
  433.6 4.5 fusion.89
  439.3 9.8 %gather_fusion.3 = bf16[512,64,128]{2,1,0:T(8,128)(2,1)} fusion(bf16[4,64,64,128]{3,2,1,0:T(8,128)(2,1)} %get-tuple-element.508, s32[512]{0:T(512)S(1)} %reshape.140), kind=kCustom, calls=%fused_computation.3.clone.1 | custom fusion | bytes 16781312 | tf_op jit(solution)/shard_map/while/body/vmap()/gather | solution.py:22
  449.1 11.4 %bitcast_add_fusion.5 = f32[16,64,4,128]{3,1,2,0:T(8,128)S(1)} fusion(f32[16,64,4,128]{3,1,2,0:T(8,128)S(1)} %get-tuple-element.486, f32[16,4,8,64,64]{4,3,2,1,0:T(8,128)} %copy-done.1, f32[16,64,4]{1,2,0:T(4,128)S(1)} %max.9, pred[16,4,8]{2,1,0:T(4,128)(4,1)S(1)} %copy.227, bf16[4,16,8,64,128]{4,3,2,1,0:T(8,128)(2,1)} %bitcast.242, ...), kind=kOutput, calls=%fused_computation.45.clone.1 | convolution fusion | flops 546308096 | bytes 21004800 | tf_op jit(solution)/shard_map/while/body/qbhgt,hqgtd->qbhd/dot_general | solution.py:81
  461.5 9.9 %gather_fusion.2 = bf16[512,64,128]{2,1,0:T(8,128)(2,1)} fusion(bf16[4,64,64,128]{3,2,1,0:T(8,128)(2,1)} %get-tuple-element.506, s32[512]{0:T(512)S(1)} %reshape.140), kind=kCustom, calls=%fused_computation.2.clone.1 | custom fusion | bytes 16781312 | tf_op jit(solution)/shard_map/while/body/vmap()/gather | solution.py:22
  471.4 5.7 bitcast_reduce_fusion.5
  477.2 4.5 fusion.89
  482.9 9.8 %gather_fusion.3 = bf16[512,64,128]{2,1,0:T(8,128)(2,1)} fusion(bf16[4,64,64,128]{3,2,1,0:T(8,128)(2,1)} %get-tuple-element.508, s32[512]{0:T(512)S(1)} %reshape.140), kind=kCustom, calls=%fused_computation.3.clone.1 | custom fusion | bytes 16781312 | tf_op jit(solution)/shard_map/while/body/vmap()/gather | solution.py:22
  492.7 11.4 %bitcast_add_fusion.5 = f32[16,64,4,128]{3,1,2,0:T(8,128)S(1)} fusion(f32[16,64,4,128]{3,1,2,0:T(8,128)S(1)} %get-tuple-element.486, f32[16,4,8,64,64]{4,3,2,1,0:T(8,128)} %copy-done.1, f32[16,64,4]{1,2,0:T(4,128)S(1)} %max.9, pred[16,4,8]{2,1,0:T(4,128)(4,1)S(1)} %copy.227, bf16[4,16,8,64,128]{4,3,2,1,0:T(8,128)(2,1)} %bitcast.242, ...), kind=kOutput, calls=%fused_computation.45.clone.1 | convolution fusion | flops 546308096 | bytes 21004800 | tf_op jit(solution)/shard_map/while/body/qbhgt,hqgtd->qbhd/dot_general | solution.py:81
  504.2 2.0 fusion.59
  508.7 29.0 %all_to_all.63 = bf16[2,1024,4,128]{3,2,0,1:T(4,128)(2,1)S(1)} all-to-all(bf16[2,1024,4,128]{3,2,0,1:T(4,128)(2,1)S(1)} %copy.177), channel_id=1, replica_groups=mesh['section'=4,'seq'=8] {'seq'}, dimensions={1} | all-to-all | bytes 4194304 | tf_op jit(solution)/shard_map/all_to_all | solution.py:138
  539.9 47.1 %collective-permute-done = bf16[2,128,32,128]{3,1,2,0:T(8,128)(2,1)} collective-permute-done((bf16[2,128,32,128]{3,1,2,0:T(8,128)(2,1)S(1)}, bf16[2,128,32,128]{3,1,2,0:T(8,128)(2,1)}, u32[]{:S(2)}, u32[]{:S(2)}) %collective-permute-start) | collective-permute-done | bytes 2097184 | tf_op jit(solution)/shard_map/ppermute | solution.py:18
  587.0 3.1 copy.180
  590.1 2.7 copy.181
  (167 shorter events, 46.7 us)
Async XLA Ops:
  3.1 39.6 %copy-start.15 = (s32[1,4,2,16]{3,2,1,0:T(2,128)S(1)}, s32[1,4,2,16]{3,2,1,0:T(2,128)}, u32[]{:S(2)}) copy-start(s32[1,4,2,16]{3,2,1,0:T(2,128)} %param.18) | copy-start | bytes 1540
  4.6 42.7 %copy-start.13 = (s32[1,4,2,16,32]{4,3,2,1,0:T(8,128)S(1)}, s32[1,4,2,16,32]{4,3,2,1,0:T(8,128)}, u32[]{:S(2)}) copy-start(s32[1,4,2,16,32]{4,3,2,1,0:T(8,128)} %param.17) | copy-start | bytes 49156
  4.6 42.8 %copy-start.16 = (s32[2]{0:T(128)S(1)}, s32[2]{0:T(128)}, u32[]{:S(2)}) copy-start(s32[2]{0:T(128)} %param.19) | copy-start | bytes 28
  4.6 31.9 %all-to-all-start.1 = ((bf16[2,128,32,128]{1,3,0,2:T(8,128)(2,1)}), bf16[2,128,32,128]{1,3,0,2:T(8,128)(2,1)S(1)}, u32[]{:S(2)}, u32[]{:S(2)}) async-start(bf16[2,128,32,128]{1,3,0,2:T(8,128)(2,1)} %copy.149), calls=%async_computation.1 | async-start | bytes 4194304 | tf_op jit(solution)/shard_map/all_to_all | solution.py:120
  38.4 31.0 %all-to-all-start = ((bf16[2,128,32,128]{3,1,0,2:T(8,128)(2,1)}), bf16[2,128,32,128]{3,1,0,2:T(8,128)(2,1)}, u32[]{:S(2)}, u32[]{:S(2)}) async-start(bf16[2,128,32,128]{3,1,0,2:T(8,128)(2,1)} %bitcast.22), calls=%async_computation | async-start | bytes 4194304 | tf_op jit(solution)/shard_map/all_to_all | solution.py:121
  48.4 57.9 %copy-start.2 = (pred[1024,1024]{0,1:T(8,128)(4,1)}, pred[1024,1024]{0,1:T(8,128)(4,1)S(1)}, u32[]{:S(2)}) copy-start(pred[1024,1024]{0,1:T(8,128)(4,1)S(1)} %iota_compare_fusion) | copy-start | bytes 3145732
  72.2 31.2 %all-to-all-start.2 = ((bf16[2,128,32,128]{3,1,0,2:T(8,128)(2,1)}), bf16[2,128,32,128]{3,1,0,2:T(8,128)(2,1)}, u32[]{:S(2)}, u32[]{:S(2)}) async-start(bf16[2,128,32,128]{3,1,0,2:T(8,128)(2,1)} %bitcast.249), calls=%async_computation.2 | async-start | bytes 4194304 | tf_op jit(solution)/shard_map/all_to_all | solution.py:122
  78.8 7.3 %copy-start.8 = (bf16[1,8,128,4,128]{4,2,3,1,0:T(8,128)(2,1)S(1)}, bf16[1,8,128,4,128]{4,2,3,1,0:T(8,128)(2,1)}, u32[]{:S(2)}) copy-start(bf16[1,8,128,4,128]{4,2,3,1,0:T(8,128)(2,1)} %get-tuple-element.295) | copy-start | bytes 3145732
  86.2 15.1 %copy-start.6 = (bf16[1,8,128,4,128]{4,2,1,3,0:T(8,128)(2,1)}, bf16[1,8,128,4,128]{4,2,1,3,0:T(8,128)(2,1)S(1)}, u32[]{:S(2)}) copy-start(bf16[1,8,128,4,128]{4,2,1,3,0:T(8,128)(2,1)S(1)} %copy.166) | copy-start | bytes 3145732
  122.9 183.6 %copy-start.14 = (f32[1024,4]{0,1:T(4,128)S(1)}, f32[1024,4]{0,1:T(4,128)}, u32[]{:S(2)}) copy-start(f32[1024,4]{0,1:T(4,128)} %get-tuple-element.238) | copy-start | bytes 49156
  122.9 183.7 %copy-start.3 = (pred[1024,1024]{0,1:T(8,128)(4,1)S(1)}, pred[1024,1024]{0,1:T(8,128)(4,1)}, u32[]{:S(2)}) copy-start(pred[1024,1024]{0,1:T(8,128)(4,1)} %copy-done.2) | copy-start | bytes 3145732
  140.0 5.7 copy-start
  145.7 10.0 %copy-start.4 = (f32[16,64,4,128]{3,1,2,0:T(8,128)S(1)}, f32[16,64,4,128]{3,1,2,0:T(8,128)}, u32[]{:S(2)}) copy-start(f32[16,64,4,128]{3,1,2,0:T(8,128)} %get-tuple-element.531) | copy-start | bytes 6291460 | tf_op jit(solution)/shard_map/while
  167.2 1.4 copy-start.5
  185.3 5.7 copy-start
  191.1 10.0 %copy-start.4 = (f32[16,64,4,128]{3,1,2,0:T(8,128)S(1)}, f32[16,64,4,128]{3,1,2,0:T(8,128)}, u32[]{:S(2)}) copy-start(f32[16,64,4,128]{3,1,2,0:T(8,128)} %get-tuple-element.531) | copy-start | bytes 6291460 | tf_op jit(solution)/shard_map/while
  212.5 1.4 copy-start.5
  230.7 5.7 copy-start
  236.4 10.0 %copy-start.4 = (f32[16,64,4,128]{3,1,2,0:T(8,128)S(1)}, f32[16,64,4,128]{3,1,2,0:T(8,128)}, u32[]{:S(2)}) copy-start(f32[16,64,4,128]{3,1,2,0:T(8,128)} %get-tuple-element.531) | copy-start | bytes 6291460 | tf_op jit(solution)/shard_map/while
  257.8 1.4 copy-start.5
  276.0 5.7 copy-start
  281.7 10.0 %copy-start.4 = (f32[16,64,4,128]{3,1,2,0:T(8,128)S(1)}, f32[16,64,4,128]{3,1,2,0:T(8,128)}, u32[]{:S(2)}) copy-start(f32[16,64,4,128]{3,1,2,0:T(8,128)} %get-tuple-element.531) | copy-start | bytes 6291460 | tf_op jit(solution)/shard_map/while
  303.1 1.4 copy-start.5
  314.3 14.2 %copy-start.7 = (bf16[1,8,128,4,128]{4,2,1,3,0:T(8,128)(2,1)S(1)}, bf16[1,8,128,4,128]{4,2,1,3,0:T(8,128)(2,1)}, u32[]{:S(2)}) copy-start(bf16[1,8,128,4,128]{4,2,1,3,0:T(8,128)(2,1)} %copy-done.6) | copy-start | bytes 3145732
  314.3 15.3 %copy-start.9 = (s32[4,16,32]{2,1,0:T(8,128)S(1)}, s32[4,16,32]{2,1,0:T(8,128)}, u32[]{:S(2)}) copy-start(s32[4,16,32]{2,1,0:T(8,128)} %get-tuple-element.474) | copy-start | bytes 24580
  314.3 15.3 %copy-start.12 = (s32[4,1,16]{2,1,0:T(1,128)S(1)}, s32[4,1,16]{2,1,0:T(1,128)}, u32[]{:S(2)}) copy-start(s32[4,1,16]{2,1,0:T(1,128)} %get-tuple-element.302) | copy-start | bytes 772
  329.6 174.6 %copy-start.11 = (f32[16,64,4]{1,0,2:T(8,128)S(1)}, f32[16,64,4]{1,0,2:T(8,128)}, u32[]{:S(2)}) copy-start(f32[16,64,4]{1,0,2:T(8,128)} %copy.163) | copy-start | bytes 49156
  330.7 9.9 %copy-start.10 = (bf16[16,64,4,128]{3,1,2,0:T(8,128)(2,1)S(1)}, bf16[16,64,4,128]{3,1,2,0:T(8,128)(2,1)}, u32[]{:S(2)}) copy-start(bf16[16,64,4,128]{3,1,2,0:T(8,128)(2,1)} %get-tuple-element.507) | copy-start | bytes 3145732 | tf_op jit(solution)/shard_map/while
  346.4 5.7 copy-start.1
  374.3 9.9 %copy-start.10 = (bf16[16,64,4,128]{3,1,2,0:T(8,128)(2,1)S(1)}, bf16[16,64,4,128]{3,1,2,0:T(8,128)(2,1)}, u32[]{:S(2)}) copy-start(bf16[16,64,4,128]{3,1,2,0:T(8,128)(2,1)} %get-tuple-element.507) | copy-start | bytes 3145732 | tf_op jit(solution)/shard_map/while
  390.0 5.7 copy-start.1
  417.9 9.9 %copy-start.10 = (bf16[16,64,4,128]{3,1,2,0:T(8,128)(2,1)S(1)}, bf16[16,64,4,128]{3,1,2,0:T(8,128)(2,1)}, u32[]{:S(2)}) copy-start(bf16[16,64,4,128]{3,1,2,0:T(8,128)(2,1)} %get-tuple-element.507) | copy-start | bytes 3145732 | tf_op jit(solution)/shard_map/while
  433.6 5.7 copy-start.1
  461.5 9.9 %copy-start.10 = (bf16[16,64,4,128]{3,1,2,0:T(8,128)(2,1)S(1)}, bf16[16,64,4,128]{3,1,2,0:T(8,128)(2,1)}, u32[]{:S(2)}) copy-start(bf16[16,64,4,128]{3,1,2,0:T(8,128)(2,1)} %get-tuple-element.507) | copy-start | bytes 3145732 | tf_op jit(solution)/shard_map/while
  477.1 5.7 copy-start.1
  538.2 48.8 %collective-permute-start = (bf16[2,128,32,128]{3,1,2,0:T(8,128)(2,1)S(1)}, bf16[2,128,32,128]{3,1,2,0:T(8,128)(2,1)}, u32[]{:S(2)}, u32[]{:S(2)}) collective-permute-start(bf16[2,128,32,128]{3,1,2,0:T(8,128)(2,1)S(1)} %bitcast.266), channel_id=1, source_target_pairs={{24,0},{0,8},{8,16},{16,24},{25,1},{1,9},{9,17},{17,25},{26,2},{2,... | collective-permute-start | bytes 6291464 | tf_op jit(solution)/shard_map/ppermute | solution.py:18
where the time goes:
time: 598 us; the launch traced here: 593 us
  local copies, waits for them, and re-layouts  217 us (36%)
  matrix products  184 us (31%)
  waiting for transfers between devices  89.1 us (15%)
  other arithmetic  55 us (9%)
  blocking collectives  29 us (5%)
  starting transfers between devices  15.9 us (3%)
    gather x24, local copies, waits for them, and re-layouts, pick_blocks(): return table[chosen]  159 us
    dot_general x8, matrix products, one_round(): jnp.einsum('qbhgt,hqgtd->qbhd', weights.astype(jnp.bfloat16), value_block...  91.2 us
    dot_general x8, matrix products, one_round(): jnp.einsum('qbhd,hqgtd->qbhgt', query_tiles, key_blocks, preferred_elemen...  47.5 us
    ppermute x1, waiting for transfers between devices, shifted(): return lax.ppermute(block, axis, route)  47.1 us
    reduce_sum x8, other arithmetic, one_round(): new_sum = run_sum * carry_scale + jnp.sum(weights, axis=(3, 4))  36.3 us
    all_to_all x1, blocking collectives, on_device(): lax.all_to_all(result, 'seq', split_axis=1, concat_axis=2, tiled=True)  29 us
    all_to_all x1, waiting for transfers between devices, on_device(): lax.all_to_all(query_rows, 'seq', split_axis=2, concat_axis=1, tiled=True)  25.4 us
    dot_general x2, matrix products, attend(): jnp.einsum('rhk,khd->rhd', own_weights.astype(jnp.bfloat16), value_local,...  24.6 us
  transfers between devices with their start and end apart: 4, of which 4 were waited for; matrix products, arithmetic and copies ran while one was open for 6% of the time, Pallas kernels for 0%

commit v1 on v0

v1 whole, which is shorter than its diff:
```python
import functools
import math

import jax
import jax.numpy as jnp
from jax import lax
from jax.experimental import pallas as pl
from jax.experimental.pallas import tpu as pltpu
from jax.sharding import PartitionSpec as P

HEADS = 32
KVH = 8
DH = 128
BLK = 64
GROUP = HEADS // KVH
ROW_TILE = 256
CHUNK = 4
TASKS = 2


def mesh_copy(src, dst, send_sem, recv_sem, section, seq):
    return pltpu.make_async_remote_copy(
        src_ref=src,
        dst_ref=dst,
        send_sem=send_sem,
        recv_sem=recv_sem,
        device_id=(section, seq),
        device_id_type=pl.DeviceIdType.MESH,
    )


def scores_of(query, keys):
    return lax.dot_general(
        query, keys, (((1,), (1,)), ((), ())), preferred_element_type=jnp.float32
    )


def fused(
    n,
    sections,
    lists,
    biases,
    queries,
    keys_new,
    values_new,
    key_cache,
    value_cache,
    out,
    qbuf,
    kbuf,
    vbuf,
    ckeys,
    cvalues,
    att,
    own_max,
    own_sum,
    own_out,
    in_send,
    in_recv,
    in_local,
    cache_sem,
    out_send,
    out_recv,
):
    spans, heads, span_len = qbuf.shape[0], qbuf.shape[1], qbuf.shape[2]
    kv_dev = kbuf.shape[1]
    rows = queries.shape[2]
    slots = lists.shape[1]
    query_blocks = span_len // BLK
    items = 2 * kv_dev + heads
    weight_scale = math.log2(math.e) / math.sqrt(DH)
    section = lax.axis_index("section")
    me = lax.axis_index("seq")
    above = lax.rem(section + 1, sections)
    below = lax.rem(section + sections - 1, sections)

    for head in range(heads):
        pltpu.make_async_copy(key_cache.at[0, head], ckeys.at[head], cache_sem.at[0, head]).start()
        pltpu.make_async_copy(
            value_cache.at[0, head], cvalues.at[head], cache_sem.at[1, head]
        ).start()

    def source(span, item, seq):
        if isinstance(item, int) and item < 2 * kv_dev:
            array = keys_new if item < kv_dev else values_new
            column = lax.div(seq * heads, GROUP) * DH + (item % kv_dev) * DH
        else:
            array = queries
            column = (seq * heads + item - 2 * kv_dev) * DH
        return array.at[0, span, :, pl.ds(pl.multiple_of(column, DH), DH)]

    def landing(span, item, seq):
        where = pl.ds(pl.multiple_of(seq * rows, rows), rows)
        if isinstance(item, int) and item < kv_dev:
            return kbuf.at[span, item, where, :]
        if isinstance(item, int) and item < 2 * kv_dev:
            return vbuf.at[span, item - kv_dev, where, :]
        return qbuf.at[span, item - 2 * kv_dev, where, :]

    def own_copy(span, item):
        return pltpu.make_async_copy(
            source(span, item, me), landing(span, item, me), in_local.at[span, item]
        )

    for span in range(spans):
        for item in range(items):
            own_copy(span, item).start()

    barrier = pltpu.get_barrier_semaphore()

    def greet(k, carry):
        @pl.when(k > 0)
        def _():
            pl.semaphore_signal(
                barrier,
                inc=1,
                device_id=(section, lax.rem(me + k, n)),
                device_id_type=pl.DeviceIdType.MESH,
            )

        for there in (above, below):
            pl.semaphore_signal(
                barrier,
                inc=1,
                device_id=(there, lax.rem(me + k, n)),
                device_id_type=pl.DeviceIdType.MESH,
            )
        return carry

    lax.fori_loop(0, n, greet, 0)
    pl.semaphore_wait(barrier, 3 * n - 1)

    def in_copy(span, item, k, seq_to, seq_from):
        return mesh_copy(
            source(span, item, seq_to),
            landing(span, item, seq_from),
            in_send.at[span, item, k],
            in_recv.at[span, item, k],
            section,
            seq_to,
        )

    for span in range(spans):
        for item in range(items):

            def send_in(k, carry):
                in_copy(span, item, k, lax.rem(me + k, n), me).start()
                return carry

            lax.fori_loop(1, n, send_in, 0)

    def await_in(span, item):
        own_copy(span, item).wait()

        def one(k, carry):
            in_copy(
                span, item, k, lax.rem(me + k, n), lax.rem(me + n - k, n)
            ).wait_recv()
            return carry

        lax.fori_loop(1, n, one, 0)

    def out_copy(span, head, k, seq_to, seq_from):
        column = pl.multiple_of((seq_from * heads + head) * DH, DH)
        return mesh_copy(
            att.at[span, head, pl.ds(pl.multiple_of(seq_to * rows, rows), rows), :],
            out.at[0, span, :, pl.ds(column, DH)],
            out_send.at[span, head, k],
            out_recv.at[span, head, k],
            above,
            seq_to,
        )

    row_at = lax.broadcasted_iota(jnp.int32, (ROW_TILE, ROW_TILE), 0)
    key_at = lax.broadcasted_iota(jnp.int32, (ROW_TILE, ROW_TILE), 1)

    def weigh(scores, top):
        return jnp.exp2((scores - top) * weight_scale)

    def own_part(span, head, kv, tile):
        start = tile * ROW_TILE
        query = qbuf[span, head, start : start + ROW_TILE, :]
        parts = []
        for piece in range(tile + 1):
            keys = kbuf[span, kv, piece * ROW_TILE : (piece + 1) * ROW_TILE, :]
            scores = scores_of(query, keys)
            if piece == tile:
                scores = jnp.where(row_at >= key_at, scores, -jnp.inf)
            parts.append(scores)
        top = jnp.max(functools.reduce(jnp.maximum, parts), axis=1, keepdims=True)
        summed, mixed = None, None
        for piece, scores in enumerate(parts):
            weights = weigh(scores, top)
            values = vbuf[span, kv, piece * ROW_TILE : (piece + 1) * ROW_TILE, :]
            product = jnp.dot(
                weights.astype(jnp.bfloat16), values, preferred_element_type=jnp.float32
            )
            summed = weights if summed is None else summed + weights
            mixed = product if mixed is None else mixed + product
        total = jnp.sum(summed, axis=1, keepdims=True)
        own_max[start : start + ROW_TILE, :] = jnp.broadcast_to(top, (ROW_TILE, DH))
        own_sum[start : start + ROW_TILE, :] = jnp.broadcast_to(total, (ROW_TILE, DH))
        own_out[start : start + ROW_TILE, :] = mixed

    def cache_part(span, head, block):
        listed = (head * spans + span) * query_blocks + block
        at = pl.ds(pl.multiple_of(block * BLK, BLK), BLK)
        query = qbuf[span, head, at, :]
        chosen = [lists[listed, i] for i in range(slots)]
        bias = biases[listed]
        parts = []
        for first in range(0, slots, CHUNK):
            keys = jnp.concatenate(
                [
                    ckeys[head, chosen[i]]
                    for i in range(first, first + CHUNK)
                ],
                axis=0,
            )
            scores = scores_of(query, keys)
            parts.append(scores + bias[first // CHUNK : first // CHUNK + 1, :])
        before = own_max[at, :][:, :1]
        top = jnp.max(functools.reduce(jnp.maximum, parts), axis=1, keepdims=True)
        top = jnp.maximum(top, before)
        summed, mixed = None, None
        for step, scores in enumerate(parts):
            weights = weigh(scores, top)
            values = jnp.concatenate(
                [
                    cvalues[head, chosen[i]]
                    for i in range(step * CHUNK, (step + 1) * CHUNK)
                ],
                axis=0,
            )
            product = jnp.dot(
                weights.astype(jnp.bfloat16), values, preferred_element_type=jnp.float32
            )
            summed = weights if summed is None else summed + weights
            mixed = product if mixed is None else mixed + product
        fade = weigh(before, top)
        total = jnp.sum(summed, axis=1, keepdims=True) + own_sum[at, :][:, :1] * fade
        return ((mixed + own_out[at, :] * fade) / total).astype(jnp.bfloat16)

    for head in range(heads):
        pltpu.make_async_copy(key_cache.at[0, head], ckeys.at[head], cache_sem.at[0, head]).wait()
        pltpu.make_async_copy(
            value_cache.at[0, head], cvalues.at[head], cache_sem.at[1, head]
        ).wait()

    for span in range(spans):
        for item in range(2 * kv_dev):
            await_in(span, item)

        def one_head(head, carry):
            kv = lax.div(head, GROUP)
            await_in(span, 2 * kv_dev + head)
            for tile in range(span_len // ROW_TILE):
                own_part(span, head, kv, tile)

            def tasks(step, inner):
                done = [cache_part(span, head, step * TASKS + t) for t in range(TASKS)]
                for t in range(TASKS):
                    at = pl.ds(pl.multiple_of((step * TASKS + t) * BLK, BLK), BLK)
                    att[span, head, at, :] = done[t]
                return inner

            lax.fori_loop(0, query_blocks // TASKS, tasks, 0)

            def send_out(k, inner):
                out_copy(span, head, k, lax.rem(me + k, n), me).start()
                return inner

            lax.fori_loop(0, n, send_out, 0)
            return carry

        lax.fori_loop(0, heads, one_head, 0)

    for span in range(spans):
        for item in range(items):

            def sent(k, carry):
                in_copy(span, item, k, lax.rem(me + k, n), me).wait_send()
                return carry

            lax.fori_loop(1, n, sent, 0)

        def head_done(head, carry):
            def both(k, inner):
                out_copy(span, head, k, lax.rem(me + k, n), me).wait_send()
                out_copy(
                    span, head, k, lax.rem(me + k, n), lax.rem(me + n - k, n)
                ).wait_recv()
                return inner

            return lax.fori_loop(0, n, both, carry)

        lax.fori_loop(0, heads, head_done, 0)


def on_device(
    queries, keys_new, values_new, key_cache, value_cache, block_lists, block_counts, visible_blocks
):
    n = lax.axis_size("seq")
    sections = lax.axis_size("section")
    spans, rows = queries.shape[1], queries.shape[2]
    heads, context = key_cache.shape[1], key_cache.shape[2]
    kv_dev = max(1, heads // GROUP)
    span_len = rows * n
    items = 2 * kv_dev + heads
    slots = block_lists.shape[4]
    smem = pl.BlockSpec(memory_space=pltpu.MemorySpace.SMEM)
    vmem = pl.BlockSpec(memory_space=pltpu.MemorySpace.VMEM)
    anywhere = pl.BlockSpec(memory_space=pl.ANY)
    usable = (jnp.arange(slots) < block_counts[0][..., None]) & (
        block_lists[0] < visible_blocks[None, :, None, None]
    )
    biases = jnp.where(usable, 0.0, -jnp.inf).astype(jnp.float32)
    biases = jnp.repeat(biases, BLK, axis=3).reshape(-1, slots // CHUNK, CHUNK * BLK)
    dma = pltpu.SemaphoreType.DMA
    return pl.pallas_call(
        functools.partial(fused, n, sections),
        out_shape=jax.ShapeDtypeStruct(queries.shape, queries.dtype),
        in_specs=[smem, vmem] + [anywhere] * 5,
        out_specs=anywhere,
        scratch_shapes=[
            pltpu.VMEM((spans, heads, span_len, DH), jnp.bfloat16),
            pltpu.VMEM((spans, kv_dev, span_len, DH), jnp.bfloat16),
            pltpu.VMEM((spans, kv_dev, span_len, DH), jnp.bfloat16),
            pltpu.VMEM((heads, context // BLK, BLK, DH), jnp.bfloat16),
            pltpu.VMEM((heads, context // BLK, BLK, DH), jnp.bfloat16),
            pltpu.VMEM((spans, heads, span_len, DH), jnp.bfloat16),
            pltpu.VMEM((span_len, DH), jnp.float32),
            pltpu.VMEM((span_len, DH), jnp.float32),
            pltpu.VMEM((span_len, DH), jnp.float32),
            dma((spans, items, n)),
            dma((spans, items, n)),
            dma((spans, items)),
            dma((2, heads)),
            dma((spans, heads, n)),
            dma((spans, heads, n)),
        ],
        compiler_params=pltpu.CompilerParams(
            collective_id=0, has_side_effects=True, vmem_limit_bytes=60 << 20
        ),
    )(
        block_lists.reshape(-1, slots),
        biases,
        queries,
        keys_new,
        values_new,
        key_cache.reshape(1, heads, context // BLK, BLK, DH),
        value_cache.reshape(1, heads, context // BLK, BLK, DH),
    )


def solution(mesh):
    return jax.shard_map(
        on_device,
        mesh=mesh,
        in_specs=(
            P("section", None, "seq", None),
            P("section", None, "seq", None),
            P("section", None, "seq", None),
            P("section", "seq", None, None),
            P("section", "seq", None, None),
            P("section", "seq", None, None, None),
            P("section", "seq", None, None),
            P(),
        ),
        out_specs=P("section", None, "seq", None),
        check_vma=False,
    )
```

time: 598 us -> 132 us (0.22)
  local copies, waits for them, and re-layouts: 217 us -> 5.24 us
  matrix products: 184 us -> 0 us
  Pallas kernels: 0 us -> 125 us
  waiting for transfers between devices: 89.1 us -> 0 us
  other arithmetic: 55 us -> 0.94 us
  blocking collectives: 29 us -> 0 us
  starting transfers between devices: 15.9 us -> 0 us
    dot_general x20 -> x0, matrix products: 184 us -> none  [the longest x8 91.2 us: one_round(): jnp.einsum('qbhgt,hqgtd->qbhd', weights.astype(jnp.bfloat16), value_block...]
    gather x24 -> x0, local copies, waits for them, and re-layouts: 159 us -> none  [pick_blocks(): return table[chosen]]
    pallas_call x0 -> x1, Pallas kernels: none -> 125 us  [on_device(): pl.pallas_call(functools.partial(fused, n, sections), out_shape=jax.Shape...]
    ppermute x1 -> x0, waiting for transfers between devices: 47.1 us -> none  [shifted(): return lax.ppermute(block, axis, route)]
    reduce_sum x9 -> x0, other arithmetic: 44 us -> none  [the longest x8 36.3 us: one_round(): new_sum = run_sum * carry_scale + jnp.sum(weights, axis=(3, 4))]
    all_to_all x3 -> x0, waiting for transfers between devices: 42 us -> none  [the longest x1 25.4 us: on_device(): lax.all_to_all(query_rows, 'seq', split_axis=2, concat_axis=1, tiled=True)]
    all_to_all x1 -> x0, blocking collectives: 29 us -> none  [on_device(): lax.all_to_all(result, 'seq', split_axis=1, concat_axis=2, tiled=True)]
    while x58 -> x0, local copies, waits for them, and re-layouts: 22.5 us -> none
  transfers between devices with their start and end apart: 4 -> 0, of which waited for: 4 -> 0; matrix products, arithmetic and copies ran while one was open for 6% -> 0% of each run, Pallas kernels for 0% -> 0%
where the time goes in v1:
time: 132 us
  Pallas kernels  125 us (95%)
  local copies, waits for them, and re-layouts  5.24 us (4%)
    pallas_call x1, Pallas kernels, on_device(): pl.pallas_call(functools.partial(fused, n, sections), out_shape=jax.Shape...  125 us
    unnamed x1, local copies, waits for them, and re-layouts  3.13 us

profile of v1, /device:TPU:0, one launch (start us, length us, event | category | flops | bytes accessed | tf_op | source)
XLA Modules:
  0.0 131.6 jit_solution(11176053882195925137)
XLA Ops:
  0.0 0.9 fusion.1
  0.9 0.6 broadcast_in_dim.15
  1.6 1.5 %reshape_reshape.3.biases = f32[128,8,256]{2,1,0:T(8,128)} reshape(f32[4,2,16,32,64]{4,3,2,1,0:T(8,128)S(1)} %broadcast_in_dim.15) | data formatting | bytes 2097152 | tf_op jit(solution)/shard_map/reshape;reshape | solution.py:318
  3.1 125.4 %shard_map.82 = bf16[1,2,128,4096]{3,2,1,0:T(8,128)(2,1)} custom-call(s32[128,32]{1,0:T(8,128)} %bitcast.12, f32[128,8,256]{2,1,0:T(8,128)} %reshape_reshape.3.biases, bf16[1,2,128,4096]{3,2,1,0:T(8,128)(2,1)} %queries.1, bf16[1,2,128,1024]{3,2,1,0:T(8,128)(2,1)} %keys_new.1, bf16[1,2,128,1024]{3,2,1,0:T(8,128)(2,1)} %values_new.1, ...), custom_call_target="tpu_custom_call" | custom-call | tf_op jit(solution)/shard_map/pallas_call | solution.py:320
  128.4 3.1 %copy.10 = bf16[1,2,128,4096]{3,2,1,0:T(8,128)(2,1)} copy(bf16[1,2,128,4096]{3,2,1,0:T(8,128)(2,1)} %shard_map.82) | data formatting | bytes 4194304

commit v2 on v1

--- a/solution.py
+++ b/solution.py
@@ -15,7 +15,7 @@
 GROUP = HEADS // KVH
 ROW_TILE = 256
 CHUNK = 4
-TASKS = 2
+TASKS = 4
 
 
 def mesh_copy(src, dst, send_sem, recv_sem, section, seq):

time: 132 us -> 126 us (0.955)
  Pallas kernels: 125 us -> 120 us
    pallas_call x1, Pallas kernels: 125 us -> 120 us  [on_device(): pl.pallas_call(functools.partial(fused, n, sections), out_shape=jax.Shape...]
where the time goes in v2:
time: 126 us
  Pallas kernels  120 us (95%)
  local copies, waits for them, and re-layouts  5.24 us (4%)
    pallas_call x1, Pallas kernels, on_device(): pl.pallas_call(functools.partial(fused, n, sections), out_shape=jax.Shape...  120 us
    unnamed x1, local copies, waits for them, and re-layouts  3.13 us

profile of v2, /device:TPU:0, one launch (start us, length us, event | category | flops | bytes accessed | tf_op | source)
XLA Modules:
  0.0 126.1 jit_solution(10153283103618306509)
XLA Ops:
  0.0 0.9 fusion.1
  0.9 0.6 broadcast_in_dim.15
  1.6 1.5 %reshape_reshape.3.biases = f32[128,8,256]{2,1,0:T(8,128)} reshape(f32[4,2,16,32,64]{4,3,2,1,0:T(8,128)S(1)} %broadcast_in_dim.15) | data formatting | bytes 2097152 | tf_op jit(solution)/shard_map/reshape;reshape | solution.py:318
  3.1 119.9 %shard_map.82 = bf16[1,2,128,4096]{3,2,1,0:T(8,128)(2,1)} custom-call(s32[128,32]{1,0:T(8,128)} %bitcast.12, f32[128,8,256]{2,1,0:T(8,128)} %reshape_reshape.3.biases, bf16[1,2,128,4096]{3,2,1,0:T(8,128)(2,1)} %queries.1, bf16[1,2,128,1024]{3,2,1,0:T(8,128)(2,1)} %keys_new.1, bf16[1,2,128,1024]{3,2,1,0:T(8,128)(2,1)} %values_new.1, ...), custom_call_target="tpu_custom_call" | custom-call | tf_op jit(solution)/shard_map/pallas_call | solution.py:320
  123.0 3.1 %copy.10 = bf16[1,2,128,4096]{3,2,1,0:T(8,128)(2,1)} copy(bf16[1,2,128,4096]{3,2,1,0:T(8,128)(2,1)} %shard_map.82) | data formatting | bytes 4194304
